TPU v7x, 32 devices: a whole 2x2x4 slice. The times are simulated.
32 devices in a mesh: groups: 2 (over x), expert: 16 (over z, y, core).
Axes of the slice: x: 2, y: 2, z: 4, core: 2. Of those that a mesh axis runs over, the one named last changes fastest.
Arguments:
- hidden_in: bfloat16 [4096, 2048], P(('groups', 'expert')), parts along dimension 0, may hold values from -6 to 6
- norm_gain: float32 [2048], replicated, may hold values from 0.1 to 1.9
- router_weight: bfloat16 [2048, 16], replicated, may hold values from -0.125 to 0.125
- expert_ids: int32 [4096, 8], P(('groups', 'expert')), parts along dimension 0, may hold values from 0 to 15, all different within a row; in each aligned block of 128 rows (0 to 127, 128 to 255, ...) at most 96 rows name the same one
- w_gate: bfloat16 [16, 2048, 768], P('expert'), may hold values from -0.125 to 0.125
- w_up: bfloat16 [16, 2048, 768], P('expert'), may hold values from -0.125 to 0.125
- w_down: bfloat16 [16, 768, 2048], P('expert'), may hold values from -0.21875 to 0.21875
Outputs:
- combined: bfloat16 [4096, 2048], P(('groups', 'expert')), parts along dimension 0
There are 2 independent parts, one for each index of `groups`. A program takes and returns all parts, laid end to end along the dimension named above; an argument that names none is the same for every part. Nothing has to cross between parts.
Inputs may be any that keep to these rules, and one draw needn't show every extreme that they name: `expert_ids`: each row names 8 different experts; within each aligned block of 128 rows (the rows of one device) no expert is named by more than 96 rows, a bound that some block reaches.
All inputs are finite; a program needn't handle non-finite values.
Results may differ from a plain program's by a relative error of at most 0.0074.
Values may be sent and summed in bfloat16 or wider, within the bound.
A program may use at most 128 MiB of HBM per device.

v0:
```python
import jax
import jax.numpy as jnp
from jax import lax
from jax.sharding import PartitionSpec as P


def local(hidden_in, norm_gain, router_weight, expert_ids, w_gate, w_up, w_down):
    tok_rows = hidden_in.shape[0]
    top_count = expert_ids.shape[1]
    num_experts = router_weight.shape[1]
    dev_count = lax.axis_size("expert")
    local_experts = w_gate.shape[0]
    cap_rows = tok_rows * top_count * 3 // (2 * num_experts)
    as_float = hidden_in.astype(jnp.float32)
    inv_rms = lax.rsqrt(jnp.mean(as_float * as_float, axis=1, keepdims=True) + 1e-06)
    normed = (as_float * inv_rms * norm_gain).astype(jnp.bfloat16)
    logits = jnp.dot(normed, router_weight, preferred_element_type=jnp.float32)
    exp_logits = jnp.exp(logits)
    expert_iota = jnp.arange(num_experts, dtype=jnp.int32)
    choice_hot = (expert_ids[:, :, None] == expert_iota[None, None, :]).astype(jnp.float32)
    picked = jnp.sum(choice_hot * exp_logits[:, None, :], axis=2)
    route_w = picked / jnp.sum(picked, axis=1, keepdims=True)
    flat_ids = expert_ids.reshape(-1)
    onehot = (flat_ids[:, None] == expert_iota[None, :]).astype(jnp.int32)
    before = jnp.cumsum(onehot, axis=0) - onehot
    slot_index = jnp.sum(before * onehot, axis=1)
    dest_index = (
        flat_ids // local_experts * cap_rows + slot_index
    ) * local_experts + flat_ids % local_experts
    token_rows = jnp.repeat(normed, top_count, axis=0)
    outgoing = (
        jnp.zeros((num_experts * cap_rows, normed.shape[1]), jnp.bfloat16)
        .at[dest_index]
        .set(token_rows)
    )
    outgoing = outgoing.reshape(dev_count, cap_rows, local_experts, normed.shape[1])
    arrived = lax.all_to_all(outgoing, "expert", split_axis=0, concat_axis=0, tiled=True)
    gate_act = jnp.einsum("smed,edf->smef", arrived, w_gate, preferred_element_type=jnp.float32)
    up_act = jnp.einsum("smed,edf->smef", arrived, w_up, preferred_element_type=jnp.float32)
    hidden = (jax.nn.silu(gate_act) * up_act).astype(jnp.bfloat16)
    returned = lax.all_to_all(
        jnp.einsum("smef,efd->smed", hidden, w_down, preferred_element_type=jnp.float32).astype(
            jnp.bfloat16
        ),
        "expert",
        split_axis=0,
        concat_axis=0,
        tiled=True,
    )
    returned = returned.reshape(num_experts * cap_rows, normed.shape[1])
    gathered = returned[dest_index].reshape(tok_rows, top_count, normed.shape[1])
    combined = jnp.sum(gathered.astype(jnp.float32) * route_w[:, :, None], axis=1).astype(
        jnp.bfloat16
    )
    return combined


def solution(mesh):
    in_specs = (
        P(("groups", "expert"), None),
        P(),
        P(),
        P(("groups", "expert"), None),
        P("expert", None, None),
        P("expert", None, None),
        P("expert", None, None),
    )
    out_specs = P(("groups", "expert"), None)
    return jax.shard_map(local, mesh=mesh, in_specs=in_specs, out_specs=out_specs, check_vma=False)
```

profile of v0, /device:TPU:15, one launch (start us, length us, event | category | flops | bytes accessed | tf_op | source)
XLA Modules:
  0.0 354.0 jit_solution(13436347442580943173)
XLA Ops:
  0.0 0.8 broadcast_multiply_fusion
  0.8 0.9 copy.28
  1.7 0.1 eq.44
  1.8 0.1 eq.40
  1.9 1.2 fusion.29
  3.2 0.1 copy.27
  3.3 0.1 mul.63
  3.4 4.5 %reduce-window.6 = s32[16,8,128]{2,1,0:T(8,128)S(1)} reduce-window(s32[16,8,128]{2,1,0:T(8,128)S(1)} %fusion.35, s32[]{:T(128)} %constant.40.clone.1), window={size=1x1x128 pad=0_0x0_0x127_0}, to_apply=%region_0.0 | reduce-window | flops 2080768 | bytes 131076 | tf_op jit(solution)/shard_map/reduce-window
  7.9 0.1 slice.10
  8.0 0.1 copy.30
  8.2 0.1 copy.31
  8.2 0.1 broadcast_add_fusion
  8.4 2.0 fusion.31
  10.4 10.7 %scatter_custom_fusion = bf16[1536,2048]{1,0:T(8,128)(2,1)} fusion(s32[1024]{0:T(1024)S(1)} %bitcast.108, bf16[]{:T(256)} %constant.38.clone.1, bf16[128,2048]{1,0:T(8,128)(2,1)} %fusion.31), kind=kCustom, calls=%fused_computation.16 | custom fusion | bytes 6815746 | tf_op jit(solution)/shard_map/scatter | solution.py:34
  21.1 144.0 %all_to_all.10 = bf16[16,96,1,2048]{3,1,2,0:T(8,128)(2,1)S(1)} all-to-all(bf16[16,96,1,2048]{3,1,2,0:T(8,128)(2,1)} %bitcast.104), channel_id=1, replica_groups=mesh['groups'=2,'expert'=16] {'expert'}, dimensions={0} | all-to-all | bytes 12582912 | tf_op jit(solution)/shard_map/all_to_all | solution.py:37
  165.1 2.7 copy-done.1
  167.7 6.6 %fusion.1 = f32[16,96,768]{2,1,0:T(8,128)} fusion(bf16[16,96,1,2048]{3,1,2,0:T(8,128)(2,1)S(1)} %all_to_all.10, bf16[1,2048,768]{2,1,0:T(8,128)(2,1)S(1)} %copy-done.4), kind=kOutput, calls=%fused_computation.4 | convolution fusion | flops 4831838208 | bytes 14155776 | tf_op jit(solution)/shard_map/smed,edf->smef/dot_general | solution.py:39
  174.3 16.8 %convert_bitcast_fusion = bf16[16,96,1,2048]{3,1,2,0:T(8,128)(2,1)} fusion(bf16[1,768,2048]{2,1,0:T(8,128)(2,1)S(1)} %copy-done, f32[16,96,768]{2,1,0:T(8,128)} %fusion.1, bf16[1,2048,768]{2,1,0:T(8,128)(2,1)} %param.11, bf16[16,96,1,2048]{3,1,2,0:T(8,128)(2,1)} %copy-done.1), kind=kOutput, calls=%fused_computation.8 | convolution fusion | flops 9673900032 | bytes 23592960 | tf_op jit(solution)/shard_map/smef,efd->smed/dot_general | solution.py:42
  191.2 5.6 %all-to-all-start.1 = ((bf16[16,96,1,2048]{3,1,2,0:T(8,128)(2,1)}), bf16[16,96,1,2048]{3,1,2,0:T(8,128)(2,1)}, u32[]{:S(2)}, u32[]{:S(2)}) async-start(bf16[16,96,1,2048]{3,1,2,0:T(8,128)(2,1)} %convert_bitcast_fusion), calls=%async_computation.1 | async-start | bytes 12582912 | tf_op jit(solution)/shard_map/all_to_all | solution.py:41
  196.8 1.3 convolution_exponential_fusion
  198.2 0.1 copy.33
  198.3 135.9 %all-to-all-done.1 = bf16[16,96,1,2048]{3,1,2,0:T(8,128)(2,1)} async-done(((bf16[16,96,1,2048]{3,1,2,0:T(8,128)(2,1)}), bf16[16,96,1,2048]{3,1,2,0:T(8,128)(2,1)}, u32[]{:S(2)}, u32[]{:S(2)}) %all-to-all-start.1) | async-done | bytes 6291488 | tf_op jit(solution)/shard_map/all_to_all | solution.py:41
  334.2 12.4 %gather_fusion = bf16[1024,2048]{1,0:T(8,128)(2,1)} fusion(bf16[1536,2048]{1,0:T(8,128)(2,1)} %bitcast.26, s32[1024]{0:T(1024)S(1)} %broadcast_clamp_fusion), kind=kCustom, calls=%fused_computation | custom fusion | bytes 8392704 | tf_op jit(solution)/shard_map/gather | solution.py:51
  346.7 7.3 %fusion = bf16[128,2048]{1,0:T(8,128)(2,1)} fusion(bf16[1024,2048]{1,0:T(8,128)(2,1)} %gather_fusion, f32[128,8]{1,0:T(8,128)S(1)} %copy.33), kind=kLoop, calls=%fused_computation.3 | loop fusion | flops 6029312 | bytes 4722688 | tf_op jit(solution)/shard_map/reduce_sum | solution.py:52
  (18 shorter events, 0.2 us)
Async XLA Ops:
  0.0 174.3 %copy-start = (bf16[1,768,2048]{2,1,0:T(8,128)(2,1)S(1)}, bf16[1,768,2048]{2,1,0:T(8,128)(2,1)}, u32[]{:S(2)}) copy-start(bf16[1,768,2048]{2,1,0:T(8,128)(2,1)} %param.13) | copy-start | bytes 9437188
  21.1 146.7 %copy-start.4 = (bf16[1,2048,768]{2,1,0:T(8,128)(2,1)S(1)}, bf16[1,2048,768]{2,1,0:T(8,128)(2,1)}, u32[]{:S(2)}) copy-start(bf16[1,2048,768]{2,1,0:T(8,128)(2,1)} %param.12) | copy-start | bytes 9437188
  165.1 2.7 copy-start.1
  191.2 5.6 %copy-start.2 = (bf16[2048,16]{0,1:T(8,128)(2,1)S(1)}, bf16[2048,16]{0,1:T(8,128)(2,1)}, u32[]{:S(2)}) copy-start(bf16[2048,16]{0,1:T(8,128)(2,1)} %param.9) | copy-start | bytes 196612
  191.2 6.9 %copy-start.3 = (s32[128,8]{0,1:T(8,128)S(1)}, s32[128,8]{0,1:T(8,128)}, u32[]{:S(2)}) copy-start(s32[128,8]{0,1:T(8,128)} %param.10) | copy-start | bytes 12292
  191.2 143.1 %all-to-all-start.1 = ((bf16[16,96,1,2048]{3,1,2,0:T(8,128)(2,1)}), bf16[16,96,1,2048]{3,1,2,0:T(8,128)(2,1)}, u32[]{:S(2)}, u32[]{:S(2)}) async-start(bf16[16,96,1,2048]{3,1,2,0:T(8,128)(2,1)} %convert_bitcast_fusion), calls=%async_computation.1 | async-start | bytes 12582912 | tf_op jit(solution)/shard_map/all_to_all | solution.py:41
where the time goes:
time: 354 us
  blocking collectives  144 us (41%)
  waiting for transfers between devices  136 us (38%)
  local copies, waits for them, and re-layouts  27.4 us (8%)
  matrix products  24.7 us (7%)
  other arithmetic  16.2 us (5%)
  starting transfers between devices  5.64 us (2%)
    all_to_all x1, blocking collectives, local(): lax.all_to_all(outgoing, 'expert', split_axis=0, concat_axis=0, tiled=True)  144 us
    all_to_all x1, waiting for transfers between devices, local(): lax.all_to_all(jnp.einsum('smef,efd->smed', hidden, w_down, preferred_ele...  136 us
    dot_general x1, matrix products, local(): jnp.einsum('smef,efd->smed', hidden, w_down, preferred_element_type=jnp.f...  16.8 us
    gather x1, local copies, waits for them, and re-layouts, local(): returned[dest_index].reshape(tok_rows, top_count, normed.shape[1])  12.4 us
    scatter x1, local copies, waits for them, and re-layouts, local(): outgoing = jnp.zeros((num_experts * cap_rows, normed.shape[1]), jnp.bfloa...  10.7 us
    reduce_sum x1, other arithmetic, local(): jnp.sum(gathered.astype(jnp.float32) * route_w[:, :, None], axis=1)  7.32 us
  transfers between devices with their start and end apart: 1, of which 1 were waited for; matrix products, arithmetic and copies ran while one was open for 0% of the time, Pallas kernels for 0%

commit v1 on v0

--- a/solution.py
+++ b/solution.py
@@ -1,7 +1,263 @@
 import jax
 import jax.numpy as jnp
 from jax import lax
+from jax.experimental import pallas as pl
+from jax.experimental.pallas import tpu as pltpu
 from jax.sharding import PartitionSpec as P
+
+RING = 8
+PLACE = {0: 0, 1: 1, 7: 2, 2: 3, 6: 4, 3: 5, 5: 6, 4: 7}
+OFFSET_AT = {place: offset for offset, place in PLACE.items()}
+
+
+def ring_kernel(
+    x_ref, gain_ref, router_ref, ids_ref, gate_hbm, up_hbm, down_hbm, out_ref,
+    gate_w, up_w, down_w, xg, yb, ys, from_left, from_right, hb, route_out, route_in, route_col,
+    load_sem, ag_s, ag_r, sx_s, sx_r, sy_s, sy_r, rs_s, rs_r, w_s, w_r,
+):
+    count = 2 * RING
+    rows = x_ref.shape[0]
+    width = x_ref.shape[1]
+    ff = gate_w.shape[1]
+    me = lax.axis_index("expert")
+    core = me % 2
+    y_at = (me // 2) % 2
+    z_at = me // 4
+    place = z_at * (1 - y_at) + (RING - 1 - z_at) * y_at
+
+    def device_at(ring_place, which_core):
+        high = ring_place // 4
+        depth = ring_place * (1 - high) + (RING - 1 - ring_place) * high
+        return (depth * 2 + high) * 2 + which_core
+
+    right = device_at((place + 1) % RING, core)
+    left = device_at((place + RING - 1) % RING, core)
+    sibling = me + 1 - 2 * core
+
+    loads = [
+        pltpu.make_async_copy(src.at[0], dst, load_sem.at[i])
+        for i, (src, dst) in enumerate(((gate_hbm, gate_w), (up_hbm, up_w), (down_hbm, down_w)))
+    ]
+    for load in loads:
+        load.start()
+
+    barrier = pltpu.get_barrier_semaphore()
+
+    @pl.loop(1, count)
+    def _(step):
+        pl.semaphore_signal(
+            barrier, inc=1, device_id={"expert": (me + step) % count},
+            device_id_type=pl.DeviceIdType.MESH,
+        )
+
+    def remote(src, dst, send, recv, device):
+        return pltpu.make_async_remote_copy(
+            src_ref=src, dst_ref=dst, send_sem=send, recv_sem=recv,
+            device_id={"expert": device}, device_id_type=pl.DeviceIdType.MESH,
+        )
+
+    as_float = x_ref[...].astype(jnp.float32)
+    inv_rms = lax.rsqrt(jnp.mean(as_float * as_float, axis=1, keepdims=True) + 1e-06)
+    normed = (as_float * inv_rms * gain_ref[...]).astype(jnp.bfloat16)
+    xg[0, 0] = normed.reshape(2, rows // 2, width)
+    pl.semaphore_wait(barrier, count - 1)
+
+    def gather_copy(way, step):
+        if way == 0:
+            src, dst, device = PLACE[step], PLACE[step + 1], right
+        else:
+            src, dst, device = PLACE[(RING - step) % RING], PLACE[RING - 1 - step], left
+        if step < 3:
+            src_ref, dst_ref = xg.at[src, 0], xg.at[dst, 0]
+        else:
+            src_ref, dst_ref = xg.at[src, 0, way], xg.at[dst, 0, way]
+        return remote(src_ref, dst_ref, ag_s.at[way, step], ag_r.at[way, step], device)
+
+    def sibling_x(offset):
+        at = PLACE[offset]
+        return remote(xg.at[at, 0], xg.at[at, 1], sx_s.at[at], sx_r.at[at], sibling)
+
+    def sibling_y(offset):
+        at = PLACE[offset]
+        return remote(yb.at[at, 1], ys.at[at], sy_s.at[at], sy_r.at[at], sibling)
+
+    gather_copy(0, 0).start()
+    gather_copy(1, 0).start()
+    sibling_x(0).start()
+
+    logits = lax.dot_general(
+        router_ref[...], normed, (((1,), (1,)), ((), ())), preferred_element_type=jnp.float32
+    )
+    exp_logits = jnp.exp(logits)
+    expert_iota = lax.broadcasted_iota(jnp.int32, logits.shape, 0)
+    chosen = expert_iota < 0
+    for k in range(ids_ref.shape[0]):
+        chosen = chosen | (ids_ref[k : k + 1, :] == expert_iota)
+    picked = jnp.where(chosen, exp_logits, 0.0)
+    route = picked / jnp.sum(picked, axis=0, keepdims=True)
+    for e in range(count):
+        route_out[e] = jnp.broadcast_to(route[e : e + 1, :], (8, rows))
+
+    def route_copy(step):
+        peer = (me + step) % count
+        return remote(route_out.at[peer], route_in.at[step], w_s.at[step], w_r.at[step], peer)
+
+    @pl.loop(1, count)
+    def _(step):
+        route_copy(step).start()
+
+    route_in[0] = route_out[me]
+
+    @pl.loop(1, count)
+    def _(step):
+        route_copy(step).wait_recv()
+
+    diagonal = lax.broadcasted_iota(jnp.int32, (rows, rows), 0) == lax.broadcasted_iota(
+        jnp.int32, (rows, rows), 1
+    )
+    for at in range(RING):
+        for lane in range(2):
+            source = device_at((place + RING - OFFSET_AT[at]) % RING, core + lane - 2 * core * lane)
+            values = route_in[(me + count - source) % count]
+            column = jnp.sum(jnp.where(diagonal, values[0:1, :], 0.0), axis=1, keepdims=True)
+            route_col[at, lane] = jnp.broadcast_to(column, (rows, rows))
+
+    def compute(at, blocks):
+        total = blocks * 2 * rows
+
+        @pl.loop(0, ff // 256)
+        def _(tile):
+            columns = pl.ds(pl.multiple_of(tile * 256, 256), 256)
+            x = xg[at : at + blocks].reshape(total, width)
+            gate = jnp.dot(x, gate_w[:, columns], preferred_element_type=jnp.float32)
+            up = jnp.dot(x, up_w[:, columns], preferred_element_type=jnp.float32)
+            hb[0:total, columns] = (gate / (1.0 + jnp.exp(-gate)) * up).astype(jnp.bfloat16)
+
+        @pl.loop(0, width // 256)
+        def _(tile):
+            columns = pl.ds(pl.multiple_of(tile * 256, 256), 256)
+            y = jnp.dot(hb[0:total, :], down_w[:, columns], preferred_element_type=jnp.float32)
+            for block in range(blocks):
+                for lane in range(2):
+                    first = (block * 2 + lane) * rows
+                    weight = route_col[at + block, lane]
+                    weight = jnp.concatenate([weight, weight], axis=1)
+                    part = (y[first : first + rows] * weight).astype(jnp.bfloat16)
+                    yb[at + block, lane, :, :, columns] = part.reshape(2, rows // 2, 256)
+
+    for load in loads:
+        load.wait()
+    sibling_x(0).wait_recv()
+    compute(0, 1)
+    sibling_y(0).start()
+
+    for step in range(3):
+        for way, offset in ((0, step + 1), (1, RING - 1 - step)):
+            gather_copy(way, step).wait_recv()
+            gather_copy(way, step + 1).start()
+            sibling_x(offset).start()
+        for offset in (step + 1, RING - 1 - step):
+            sibling_x(offset).wait_recv()
+        compute(2 * step + 1, 2)
+        for offset in (step + 1, RING - 1 - step):
+            sibling_y(offset).start()
+
+    gather_copy(0, 3).wait_recv()
+    gather_copy(1, 3).wait_recv()
+    sibling_x(4).start()
+
+    incoming = (from_left, from_right)
+
+    def reduce_copy(way, half, hops):
+        at = PLACE[RING - hops if way == 0 else hops]
+        into = incoming[way]
+        number = hops * 2 + half
+        return remote(
+            yb.at[at, 0, half], into.at[hops - 1, half],
+            rs_s.at[way, number], rs_r.at[way, number], right if way == 0 else left,
+        )
+
+    def own_sum(at, half):
+        return yb[at, 0, half].astype(jnp.float32) + ys[at, half].astype(jnp.float32)
+
+    def reduce_start(way, half, hops, arrived):
+        at = PLACE[RING - hops if way == 0 else hops]
+        total = own_sum(at, half)
+        if arrived:
+            reduce_copy(way, half, hops + 1).wait_recv()
+            total = total + incoming[way][hops, half].astype(jnp.float32)
+        yb[at, 0, half] = total.astype(jnp.bfloat16)
+        reduce_copy(way, half, hops).start()
+
+    sibling_y(5).wait_recv()
+    reduce_start(0, 1, 3, False)
+    sibling_y(3).wait_recv()
+    reduce_start(1, 0, 3, False)
+    sibling_x(4).wait_recv()
+    compute(7, 1)
+    sibling_y(4).start()
+    for offset in (0, 1, 2, 6, 7, 4):
+        sibling_y(offset).wait_recv()
+    reduce_start(0, 0, 4, False)
+    reduce_start(1, 1, 4, False)
+    for late, hops in ((0, 2), (1, 3), (0, 1), (1, 2), (1, 1)):
+        reduce_start(0, 1 - late, hops, True)
+        reduce_start(1, late, hops, True)
+    for half in range(2):
+        total = own_sum(0, half)
+        for way in range(2):
+            reduce_copy(way, half, 1).wait_recv()
+            total = total + incoming[way][0, half].astype(jnp.float32)
+        out_ref[half * (rows // 2) : (half + 1) * (rows // 2), :] = total.astype(jnp.bfloat16)
+
+    for way in range(2):
+        for step in range(4):
+            gather_copy(way, step).wait_send()
+        for hops in (1, 2, 3):
+            for half in range(2):
+                reduce_copy(way, half, hops).wait_send()
+        reduce_copy(way, way, 4).wait_send()
+    for offset in range(RING):
+        sibling_x(offset).wait_send()
+        sibling_y(offset).wait_send()
+
+    @pl.loop(1, count)
+    def _(step):
+        route_copy(step).wait_send()
+
+
+def ring_local(hidden_in, norm_gain, router_weight, expert_ids, w_gate, w_up, w_down):
+    rows, width = hidden_in.shape
+    ff = w_gate.shape[2]
+    half = rows // 2
+    vmem = pl.BlockSpec(memory_space=pltpu.VMEM)
+    hbm = pl.BlockSpec(memory_space=pl.ANY)
+    dma = pltpu.SemaphoreType.DMA
+    return pl.pallas_call(
+        ring_kernel,
+        out_shape=jax.ShapeDtypeStruct((rows, width), jnp.bfloat16),
+        in_specs=[vmem, vmem, vmem, vmem, hbm, hbm, hbm],
+        out_specs=vmem,
+        scratch_shapes=[
+            pltpu.VMEM((width, ff), jnp.bfloat16),
+            pltpu.VMEM((width, ff), jnp.bfloat16),
+            pltpu.VMEM((ff, width), jnp.bfloat16),
+            pltpu.VMEM((RING, 2, 2, half, width), jnp.bfloat16),
+            pltpu.VMEM((RING, 2, 2, half, width), jnp.bfloat16),
+            pltpu.VMEM((RING, 2, half, width), jnp.bfloat16),
+            pltpu.VMEM((4, 2, half, width), jnp.bfloat16),
+            pltpu.VMEM((4, 2, half, width), jnp.bfloat16),
+            pltpu.VMEM((4 * rows, ff), jnp.bfloat16),
+            pltpu.VMEM((2 * RING, 8, rows), jnp.float32),
+            pltpu.VMEM((2 * RING, 8, rows), jnp.float32),
+            pltpu.VMEM((RING, 2, rows, rows), jnp.float32),
+            dma((3,)), dma((2, 4)), dma((2, 4)), dma((RING,)), dma((RING,)), dma((RING,)),
+            dma((RING,)), dma((2, 10)), dma((2, 10)), dma((2 * RING,)), dma((2 * RING,)),
+        ],
+        compiler_params=pltpu.CompilerParams(
+            collective_id=0, has_side_effects=True, vmem_limit_bytes=56 * 1024 * 1024
+        ),
+    )(hidden_in, norm_gain.reshape(1, width), router_weight.T, expert_ids.T, w_gate, w_up, w_down)
 
 
 def local(hidden_in, norm_gain, router_weight, expert_ids, w_gate, w_up, w_down):
@@ -66,4 +322,6 @@
         P("expert", None, None),
     )
     out_specs = P(("groups", "expert"), None)
-    return jax.shard_map(local, mesh=mesh, in_specs=in_specs, out_specs=out_specs, check_vma=False)
+    ringed = mesh.shape["expert"] == 2 * RING
+    body = ring_local if ringed else local
+    return jax.shard_map(body, mesh=mesh, in_specs=in_specs, out_specs=out_specs, check_vma=False)

time: 354 us -> 113 us (0.32)
  the two profiles are of different devices: /device:TPU:15 before, /device:TPU:0 now
where the time goes in v1:
time: 113 us
  Pallas kernels  111 us (98%)
  local copies, waits for them, and re-layouts  1.88 us (2%)
    pallas_call x1, Pallas kernels, ring_local(): pl.pallas_call(ring_kernel, out_shape=jax.ShapeDtypeStruct((rows, width),...  111 us

profile of v1, /device:TPU:0, one launch (start us, length us, event | category | flops | bytes accessed | tf_op | source)
XLA Modules:
  0.0 113.2 jit_solution(15454651713479328095)
XLA Ops:
  0.0 111.3 %shard_map.73 = bf16[128,2048]{1,0:T(8,128)(2,1)} custom-call(bf16[128,2048]{1,0:T(8,128)(2,1)} %x_ref.1, f32[1,2048]{1,0:T(1,128)} %bitcast.4, bf16[16,2048]{1,0:T(8,128)(2,1)} %bitcast.3, s32[8,128]{1,0:T(8,128)} %bitcast.5, bf16[1,2048,768]{2,1,0:T(8,128)(2,1)} %gate_hbm.1, bf16[1,2048,768]{2,1,0:T(8,128)(2,1)} %up_hbm.1, bf16[1,768,2048]{2,1,0:T(8,128)(2,1)} %down_hbm.1), custom_call_target="tpu_custom_call" | custom-call | tf_op jit(solution)/shard_map/pallas_call | solution.py:236
  111.3 1.9 %copy.9 = bf16[128,2048]{1,0:T(8,128)(2,1)} copy(bf16[128,2048]{1,0:T(8,128)(2,1)} %shard_map.73) | data formatting | bytes 1048576

commit v2 on v0

--- a/solution.py
+++ b/solution.py
@@ -1,7 +1,306 @@
 import jax
 import jax.numpy as jnp
 from jax import lax
+from jax.experimental import pallas as pl
+from jax.experimental.pallas import tpu as pltpu
 from jax.sharding import PartitionSpec as P
+
+RING = 8
+FF_TILE = 768
+OUT_TILE = 1024
+
+
+def spot(offset, half):
+    if offset == 0:
+        return 0, half
+    if offset == 4:
+        return 7, half
+    if offset < 4:
+        return 2 * offset - 1 + half, 0
+    return 2 * (RING - offset) - half, 1
+
+
+def ring_kernel(
+    x_ref, gain_ref, router_ref, ids_ref, gate_hbm, up_hbm, down_hbm, out_ref,
+    gate_w, up_w, down_w, xg, yb, ys, from_left, from_right, hb, routes, route_col, out_buf,
+    load_sem, ag_s, ag_r, sx_s, sx_r, sy_s, sy_r, rs_s, rs_r, rt_s, rt_r, rx_s, rx_r, out_sem,
+):
+    rows = x_ref.shape[0]
+    width = x_ref.shape[1]
+    ff = gate_w.shape[1]
+    half_rows = rows // 2
+    total = 2 * rows
+    me = lax.axis_index("expert")
+    core = me % 2
+    y_at = (me // 2) % 2
+    z_at = me // 4
+    place = z_at * (1 - y_at) + (RING - 1 - z_at) * y_at
+
+    def device_at(ring_place):
+        high = ring_place // 4
+        depth = ring_place * (1 - high) + (RING - 1 - ring_place) * high
+        return (depth * 2 + high) * 2 + core
+
+    right = device_at((place + 1) % RING)
+    left = device_at((place + RING - 1) % RING)
+    sibling = me + 1 - 2 * core
+    toward = (right, left)
+
+    barrier = pltpu.get_barrier_semaphore()
+    for device in (right, left, sibling):
+        pl.semaphore_signal(
+            barrier, inc=1, device_id={"expert": device}, device_id_type=pl.DeviceIdType.MESH
+        )
+
+    loads = [
+        pltpu.make_async_copy(src.at[0], dst, load_sem.at[i])
+        for i, (src, dst) in enumerate(((gate_hbm, gate_w), (up_hbm, up_w), (down_hbm, down_w)))
+    ]
+    for load in loads:
+        load.start()
+
+    def remote(src, dst, send, recv, device):
+        return pltpu.make_async_remote_copy(
+            src_ref=src, dst_ref=dst, send_sem=send, recv_sem=recv,
+            device_id={"expert": device}, device_id_type=pl.DeviceIdType.MESH,
+        )
+
+    def offset_of(way, hop):
+        return hop if way == 0 else (RING - hop) % RING
+
+    def gather_copy(way, hop, late):
+        half = late if way == 0 else 1 - late
+        unit, at = spot(offset_of(way, hop - 1), half)
+        next_unit, next_at = spot(offset_of(way, hop), half)
+        number = (hop - 1) * 2 + late
+        return remote(
+            xg.at[unit, 0, at], xg.at[next_unit, 0, next_at],
+            ag_s.at[way, number], ag_r.at[way, number], toward[way],
+        )
+
+    def sibling_x(unit, way):
+        number = unit * 2 + way
+        return remote(
+            xg.at[unit, 0, way], xg.at[unit, 1, way], sx_s.at[number], sx_r.at[number], sibling
+        )
+
+    def sibling_y(unit):
+        return remote(yb.at[unit, 1], ys.at[unit], sy_s.at[unit], sy_r.at[unit], sibling)
+
+    def route_copy(way, hop):
+        return remote(
+            routes.at[offset_of(way, hop - 1), 0], routes.at[offset_of(way, hop), 0],
+            rt_s.at[way, hop - 1], rt_r.at[way, hop - 1], toward[way],
+        )
+
+    def sibling_route(offset):
+        return remote(
+            routes.at[offset, 0], routes.at[offset, 1], rx_s.at[offset], rx_r.at[offset], sibling
+        )
+
+    as_float = x_ref[...].astype(jnp.float32)
+    inv_rms = lax.rsqrt(jnp.mean(as_float * as_float, axis=1, keepdims=True) + 1e-06)
+    normed = (as_float * inv_rms * gain_ref[...]).astype(jnp.bfloat16)
+    xg[0, 0] = normed.reshape(2, half_rows, width)
+    pl.semaphore_wait(barrier, 3)
+
+    for late in range(2):
+        for way in range(2):
+            gather_copy(way, 1, late).start()
+    for way in range(2):
+        sibling_x(0, way).start()
+
+    logits = lax.dot_general(
+        router_ref[...], normed, (((1,), (1,)), ((), ())), preferred_element_type=jnp.float32
+    )
+    exp_logits = jnp.exp(logits)
+    expert_iota = lax.broadcasted_iota(jnp.int32, logits.shape, 0)
+    chosen = expert_iota < 0
+    for k in range(ids_ref.shape[0]):
+        chosen = chosen | (ids_ref[k : k + 1, :] == expert_iota)
+    picked = jnp.where(chosen, exp_logits, 0.0)
+    routes[0, 0] = picked / jnp.sum(picked, axis=0, keepdims=True)
+    route_copy(0, 1).start()
+    route_copy(1, 1).start()
+    sibling_route(0).start()
+
+    diagonal = lax.broadcasted_iota(jnp.int32, (rows, rows), 0) == lax.broadcasted_iota(
+        jnp.int32, (rows, rows), 1
+    )
+
+    def columns_of(offset):
+        sibling_route(offset).wait_recv()
+        for lane in range(2):
+            values = routes[offset, lane, pl.ds(me, 1), :]
+            column = jnp.sum(jnp.where(diagonal, values, 0.0), axis=1, keepdims=True)
+            spread = jnp.broadcast_to(column, (rows, rows))
+            for half in range(2):
+                unit, way = spot(offset, half)
+                route_col[unit, lane, way] = spread[half * half_rows : (half + 1) * half_rows]
+
+    def compute(unit):
+        for way in range(2):
+            sibling_x(unit, way).wait_recv()
+
+        @pl.loop(0, ff // FF_TILE)
+        def _(tile):
+            columns = pl.ds(pl.multiple_of(tile * FF_TILE, FF_TILE), FF_TILE)
+            x = xg[unit].reshape(total, width)
+            gate = jnp.dot(x, gate_w[:, columns], preferred_element_type=jnp.float32)
+            up = jnp.dot(x, up_w[:, columns], preferred_element_type=jnp.float32)
+            hb[:, columns] = (gate / (1.0 + jnp.exp(-gate)) * up).astype(jnp.bfloat16)
+
+        @pl.loop(0, width // OUT_TILE)
+        def _(tile):
+            columns = pl.ds(pl.multiple_of(tile * OUT_TILE, OUT_TILE), OUT_TILE)
+            y = jnp.dot(hb[...], down_w[:, columns], preferred_element_type=jnp.float32)
+            for lane in range(2):
+                for way in range(2):
+                    first = (lane * 2 + way) * half_rows
+                    weight = route_col[unit, lane, way]
+                    weight = jnp.concatenate([weight] * (OUT_TILE // rows), axis=1)
+                    part = y[first : first + half_rows] * weight
+                    yb[unit, lane, way, :, columns] = part.astype(jnp.bfloat16)
+
+        sibling_y(unit).start()
+
+    incoming = (from_left, from_right)
+
+    def reduce_copy(way, half, hops):
+        unit, at = spot(RING - hops if way == 0 else hops, half)
+        number = hops * 2 + half
+        return remote(
+            yb.at[unit, 0, at], incoming[way].at[hops - 1, half],
+            rs_s.at[way, number], rs_r.at[way, number], toward[way],
+        )
+
+    def own_sum(unit, way):
+        return yb[unit, 0, way].astype(jnp.float32) + ys[unit, way].astype(jnp.float32)
+
+    def reduce_start(way, half, hops, arrived):
+        unit, at = spot(RING - hops if way == 0 else hops, half)
+        value = own_sum(unit, at)
+        if arrived:
+            reduce_copy(way, half, hops + 1).wait_recv()
+            value = value + incoming[way][hops, half].astype(jnp.float32)
+        yb[unit, 0, at] = value.astype(jnp.bfloat16)
+        reduce_copy(way, half, hops).start()
+
+    for hop in range(1, 4):
+        for way in range(2):
+            gather_copy(way, hop, 0).wait_recv()
+            gather_copy(way, hop + 1, 0).start()
+            sibling_x(2 * hop - 1, way).start()
+        for way in range(2):
+            route_copy(way, hop).wait_recv()
+            if way == 0 or hop < 3:
+                route_copy(way, hop + 1).start()
+            sibling_route(offset_of(way, hop)).start()
+        if hop == 1:
+            columns_of(0)
+            for load in loads:
+                load.wait()
+        compute(2 * hop - 2)
+        columns_of(hop)
+        columns_of(RING - hop)
+        if hop == 3:
+            compute(5)
+        for way in range(2):
+            gather_copy(way, hop, 1).wait_recv()
+            if hop < 3:
+                gather_copy(way, hop + 1, 1).start()
+            sibling_x(2 * hop, way).start()
+        if hop < 3:
+            compute(2 * hop - 1)
+
+    route_copy(0, 4).wait_recv()
+    sibling_route(4).start()
+    for unit in range(6):
+        sibling_y(unit).wait_recv()
+    reduce_start(0, 1, 3, False)
+    reduce_start(1, 0, 3, False)
+    for way in range(2):
+        gather_copy(way, 4, 0).wait_recv()
+        sibling_x(7, way).start()
+    columns_of(4)
+    compute(7)
+    sibling_y(7).wait_recv()
+    reduce_start(0, 0, 4, False)
+    reduce_start(1, 1, 4, False)
+    reduce_start(0, 1, 2, True)
+    reduce_start(1, 0, 2, True)
+    compute(6)
+    sibling_y(6).wait_recv()
+    for late, hops in ((1, 3), (0, 1), (1, 2), (1, 1)):
+        reduce_start(0, 1 - late, hops, True)
+        reduce_start(1, late, hops, True)
+
+    def out_copy(half):
+        return pltpu.make_async_copy(
+            out_buf.at[half], out_ref.at[pl.ds(half * half_rows, half_rows)], out_sem.at[half]
+        )
+
+    for half in range(2):
+        value = own_sum(0, half)
+        for way in range(2):
+            reduce_copy(way, half, 1).wait_recv()
+            value = value + incoming[way][0, half].astype(jnp.float32)
+        out_buf[half] = value.astype(jnp.bfloat16)
+        out_copy(half).start()
+
+    for way in range(2):
+        for hop in range(1, 5):
+            for late in range(2 if hop < 4 else 1):
+                gather_copy(way, hop, late).wait_send()
+            if way == 0 or hop < 4:
+                route_copy(way, hop).wait_send()
+        for hops in (1, 2, 3):
+            for half in range(2):
+                reduce_copy(way, half, hops).wait_send()
+        reduce_copy(way, way, 4).wait_send()
+    for unit in range(RING):
+        for way in range(2):
+            sibling_x(unit, way).wait_send()
+        sibling_y(unit).wait_send()
+        sibling_route(unit).wait_send()
+    for half in range(2):
+        out_copy(half).wait()
+
+
+def ring_local(hidden_in, norm_gain, router_weight, expert_ids, w_gate, w_up, w_down):
+    rows, width = hidden_in.shape
+    ff = w_gate.shape[2]
+    half = rows // 2
+    count = router_weight.shape[1]
+    vmem = pl.BlockSpec(memory_space=pltpu.VMEM)
+    hbm = pl.BlockSpec(memory_space=pl.ANY)
+    dma = pltpu.SemaphoreType.DMA
+    return pl.pallas_call(
+        ring_kernel,
+        out_shape=jax.ShapeDtypeStruct((rows, width), jnp.bfloat16),
+        in_specs=[vmem, vmem, vmem, vmem, hbm, hbm, hbm],
+        out_specs=hbm,
+        scratch_shapes=[
+            pltpu.VMEM((width, ff), jnp.bfloat16),
+            pltpu.VMEM((width, ff), jnp.bfloat16),
+            pltpu.VMEM((ff, width), jnp.bfloat16),
+            pltpu.VMEM((RING, 2, 2, half, width), jnp.bfloat16),
+            pltpu.VMEM((RING, 2, 2, half, width), jnp.bfloat16),
+            pltpu.VMEM((RING, 2, half, width), jnp.bfloat16),
+            pltpu.VMEM((4, 2, half, width), jnp.bfloat16),
+            pltpu.VMEM((4, 2, half, width), jnp.bfloat16),
+            pltpu.VMEM((2 * rows, ff), jnp.bfloat16),
+            pltpu.VMEM((RING, 2, count, rows), jnp.float32),
+            pltpu.VMEM((RING, 2, 2, half, rows), jnp.float32),
+            pltpu.VMEM((2, half, width), jnp.bfloat16),
+            dma((3,)), dma((2, 8)), dma((2, 8)), dma((2 * RING,)), dma((2 * RING,)),
+            dma((RING,)), dma((RING,)), dma((2, 10)), dma((2, 10)), dma((2, 4)), dma((2, 4)),
+            dma((RING,)), dma((RING,)), dma((2,)),
+        ],
+        compiler_params=pltpu.CompilerParams(
+            collective_id=0, has_side_effects=True, vmem_limit_bytes=56 * 1024 * 1024
+        ),
+    )(hidden_in, norm_gain.reshape(1, width), router_weight.T, expert_ids.T, w_gate, w_up, w_down)
 
 
 def local(hidden_in, norm_gain, router_weight, expert_ids, w_gate, w_up, w_down):
@@ -66,4 +365,6 @@
         P("expert", None, None),
     )
     out_specs = P(("groups", "expert"), None)
-    return jax.shard_map(local, mesh=mesh, in_specs=in_specs, out_specs=out_specs, check_vma=False)
+    ringed = mesh.shape["expert"] == 2 * RING
+    body = ring_local if ringed else local
+    return jax.shard_map(body, mesh=mesh, in_specs=in_specs, out_specs=out_specs, check_vma=False)

time: 354 us -> 93.3 us (0.26)
  the two profiles are of different devices: /device:TPU:15 before, /device:TPU:0 now
where the time goes in v2:
time: 93.3 us; the launch traced here: 93.1 us
  Pallas kernels  91.2 us (98%)
  local copies, waits for them, and re-layouts  1.88 us (2%)
    pallas_call x1, Pallas kernels, ring_local(): pl.pallas_call(ring_kernel, out_shape=jax.ShapeDtypeStruct((rows, width),...  91.2 us
    unnamed x1, local copies, waits for them, and re-layouts  1.88 us

profile of v2, /device:TPU:0, one launch (start us, length us, event | category | flops | bytes accessed | tf_op | source)
XLA Modules:
  0.0 93.1 jit_solution(10065276981760081770)
XLA Ops:
  0.0 91.2 %shard_map.73 = bf16[128,2048]{1,0:T(8,128)(2,1)} custom-call(bf16[128,2048]{1,0:T(8,128)(2,1)} %x_ref.1, f32[1,2048]{1,0:T(1,128)} %bitcast.4, bf16[16,2048]{1,0:T(8,128)(2,1)} %bitcast.3, s32[8,128]{1,0:T(8,128)} %bitcast.5, bf16[1,2048,768]{2,1,0:T(8,128)(2,1)} %gate_hbm.1, bf16[1,2048,768]{2,1,0:T(8,128)(2,1)} %up_hbm.1, bf16[1,768,2048]{2,1,0:T(8,128)(2,1)} %down_hbm.1), custom_call_target="tpu_custom_call" | custom-call | tf_op jit(solution)/shard_map/pallas_call | solution.py:278
  91.2 1.9 %copy.9 = bf16[128,2048]{1,0:T(8,128)(2,1)} copy(bf16[128,2048]{1,0:T(8,128)(2,1)} %shard_map.73) | data formatting | bytes 1048576

commit v3 on v2

--- a/solution.py
+++ b/solution.py
@@ -7,7 +7,7 @@
 
 RING = 8
 FF_TILE = 768
-OUT_TILE = 1024
+OUT_TILE = 2048
 
 
 def spot(offset, half):
@@ -56,8 +56,6 @@
         pltpu.make_async_copy(src.at[0], dst, load_sem.at[i])
         for i, (src, dst) in enumerate(((gate_hbm, gate_w), (up_hbm, up_w), (down_hbm, down_w)))
     ]
-    for load in loads:
-        load.start()
 
     def remote(src, dst, send, recv, device):
         return pltpu.make_async_remote_copy(
@@ -109,6 +107,8 @@
             gather_copy(way, 1, late).start()
     for way in range(2):
         sibling_x(0, way).start()
+    for load in loads:
+        load.start()
 
     logits = lax.dot_general(
         router_ref[...], normed, (((1,), (1,)), ((), ())), preferred_element_type=jnp.float32
@@ -224,11 +224,11 @@
         sibling_x(7, way).start()
     columns_of(4)
     compute(7)
+    reduce_start(0, 1, 2, True)
+    reduce_start(1, 0, 2, True)
     sibling_y(7).wait_recv()
     reduce_start(0, 0, 4, False)
     reduce_start(1, 1, 4, False)
-    reduce_start(0, 1, 2, True)
-    reduce_start(1, 0, 2, True)
     compute(6)
     sibling_y(6).wait_recv()
     for late, hops in ((1, 3), (0, 1), (1, 2), (1, 1)):

time: 93.3 us -> 92.1 us (0.987)
  Pallas kernels: 91.2 us -> 90 us
    pallas_call x1, Pallas kernels: 91.2 us -> 90 us  [ring_local(): pl.pallas_call(ring_kernel, out_shape=jax.ShapeDtypeStruct((rows, width),...]
where the time goes in v3:
time: 92.1 us; the launch traced here: 91.9 us
  Pallas kernels  90 us (98%)
  local copies, waits for them, and re-layouts  1.88 us (2%)
    pallas_call x1, Pallas kernels, ring_local(): pl.pallas_call(ring_kernel, out_shape=jax.ShapeDtypeStruct((rows, width),...  90 us
    unnamed x1, local copies, waits for them, and re-layouts  1.88 us

profile of v3, /device:TPU:0, one launch (start us, length us, event | category | flops | bytes accessed | tf_op | source)
XLA Modules:
  0.0 91.9 jit_solution(16276557420765028336)
XLA Ops:
  0.0 90.0 %shard_map.73 = bf16[128,2048]{1,0:T(8,128)(2,1)} custom-call(bf16[128,2048]{1,0:T(8,128)(2,1)} %x_ref.1, f32[1,2048]{1,0:T(1,128)} %bitcast.4, bf16[16,2048]{1,0:T(8,128)(2,1)} %bitcast.3, s32[8,128]{1,0:T(8,128)} %bitcast.5, bf16[1,2048,768]{2,1,0:T(8,128)(2,1)} %gate_hbm.1, bf16[1,2048,768]{2,1,0:T(8,128)(2,1)} %up_hbm.1, bf16[1,768,2048]{2,1,0:T(8,128)(2,1)} %down_hbm.1), custom_call_target="tpu_custom_call" | custom-call | tf_op jit(solution)/shard_map/pallas_call | solution.py:278
  90.1 1.9 %copy.9 = bf16[128,2048]{1,0:T(8,128)(2,1)} copy(bf16[128,2048]{1,0:T(8,128)(2,1)} %shard_map.73) | data formatting | bytes 1048576
